TPU v7x, 128 devices: a whole 4x4x4 slice. The times are simulated.
128 devices in a mesh: section: 2 (over z_hi), expert: 8 (over y, z_lo), dp: 8 (over x, core).
Axes of the slice: x: 4, y: 4, z: 4 (z_hi: 2, z_lo: 2; z = z_hi * 2 + z_lo), core: 2. Of those that a mesh axis runs over, the one named last changes fastest.
Arguments:
- inputs: bfloat16 [2, 512, 3072], P(None, ('expert', 'dp')), may hold values from -6 to 6
- cotangent: bfloat16 [2, 512, 3072], P(None, ('expert', 'dp')), may hold values from -6 to 6
- norm_gain: bfloat16 [2, 3072], P('section'), may hold values from 0.5 to 1.5
- router: bfloat16 [2, 3072, 8], P('section'), may hold values from -0.109375 to 0.109375
- w_gate: bfloat16 [2, 8, 3072, 8192], P('section', 'expert', None, 'dp'), may hold values from -0.109375 to 0.109375
- w_up: bfloat16 [2, 8, 3072, 8192], P('section', 'expert', None, 'dp'), may hold values from -0.109375 to 0.109375
- w_down: bfloat16 [2, 8, 8192, 3072], P('section', 'expert', 'dp'), may hold values from -0.0625 to 0.0625
- routes: int32 [2, 2, 512, 2], P('section', None, ('expert', 'dp')), may hold values from 0 to 7, as said below
Outputs:
- acts: bfloat16 [2, 2, 512, 3072], P('section', None, ('expert', 'dp'))
- grads: bfloat16 [2, 2, 512, 3072], P('section', None, ('expert', 'dp'))
- router_grad: float32 [2, 3072, 8], P('section')
Inputs may be any that keep to these rules, and one draw needn't show every extreme that they name: `routes`: the two experts of a token differ. For each layer and micro-batch, the 8 tokens of one device name no expert more than 3 times, and one expert, the same on all devices for that layer and micro-batch, exactly 3 times.
All inputs are finite; a program needn't handle non-finite values.
Results may differ from a plain program's by a relative error of at most 0.017.
Values may be sent and summed in bfloat16 or wider, within the bound.
A program may use at most 128 MiB of HBM per device.

v0:
```python
import jax
import jax.numpy as jnp
from jax import lax
from jax.sharding import PartitionSpec as P

EPSILON = 1e-05


def passed_along(block, axis, distance):
    devices = range(lax.axis_size(axis))
    route = [(i - distance, i) for i in devices if i - distance in devices]
    return lax.ppermute(block, axis, route)


def norm_rows(layer_in, gain_row):
    values = layer_in.astype(jnp.float32)
    inv_rms = lax.rsqrt(jnp.mean(values * values, axis=-1, keepdims=True) + EPSILON)
    return (values, inv_rms, (values * inv_rms * gain_row).astype(jnp.bfloat16))


def gate_probs(hidden, router_w, picks):
    logits = jnp.dot(hidden, router_w, preferred_element_type=jnp.float32)
    chosen = jnp.take_along_axis(logits, picks, axis=1)
    logit_gap = chosen[:, 0] - chosen[:, 1]
    return jnp.stack([jax.nn.sigmoid(logit_gap), jax.nn.sigmoid(-logit_gap)], axis=1)


def slot_table(picks, experts, capacity):
    flat_pick = picks.reshape(-1)
    onehot = (flat_pick[:, None] == jnp.arange(experts, dtype=jnp.int32)[None, :]).astype(jnp.int32)
    earlier = jnp.cumsum(onehot, axis=0) - onehot
    slot_pos = jnp.sum(earlier * onehot, axis=1)
    target = flat_pick * capacity + slot_pos
    return target[:, None] == jnp.arange(experts * capacity, dtype=jnp.int32)[None, :]


def deliver(outgoing, experts, capacity):
    model_width = outgoing.shape[1]
    grouped = outgoing.reshape(experts, capacity, model_width)
    tiled = jnp.repeat(grouped, lax.axis_size("dp"), axis=0)
    arrived = lax.all_to_all(tiled, ("expert", "dp"), split_axis=0, concat_axis=0, tiled=True)
    return arrived.reshape(-1, model_width)


def collect(partial_out, experts, capacity):
    model_width = partial_out.shape[1]
    replicas = lax.axis_size("dp")
    returned = lax.all_to_all(
        partial_out.reshape(experts * replicas, capacity, model_width),
        ("expert", "dp"),
        split_axis=0,
        concat_axis=0,
        tiled=True,
    )
    summed = jnp.sum(
        returned.reshape(experts, replicas, capacity, model_width).astype(jnp.float32), axis=1
    )
    return summed.reshape(experts * capacity, model_width)


def send_rows(placing, row_values):
    grouped = lax.dot_general(
        placing.astype(jnp.bfloat16),
        row_values,
        (((0,), (0,)), ((), ())),
        preferred_element_type=jnp.float32,
    )
    return grouped.astype(jnp.bfloat16)


def forward_layer(layer_in, picks, gain_row, router_w, gate_w, up_w, down_w, experts, capacity):
    values, inv_rms, hidden = norm_rows(layer_in, gain_row)
    gate_prob = gate_probs(hidden, router_w, picks)
    placing = slot_table(picks, experts, capacity)
    arrived = deliver(
        send_rows(placing, jnp.repeat(hidden, picks.shape[1], axis=0)), experts, capacity
    )
    gate_pre = jnp.dot(arrived, gate_w, preferred_element_type=jnp.float32)
    up_pre = jnp.dot(arrived, up_w, preferred_element_type=jnp.float32)
    active = (gate_pre * jax.nn.sigmoid(gate_pre) * up_pre).astype(jnp.bfloat16)
    partial_out = jnp.dot(active, down_w, preferred_element_type=jnp.float32).astype(jnp.bfloat16)
    summed = collect(partial_out, experts, capacity)
    picked = jnp.dot(placing.astype(jnp.float32), summed, precision=lax.Precision.HIGHEST)
    picked = picked.reshape(layer_in.shape[0], picks.shape[1], -1)
    layer_out = (values + jnp.sum(gate_prob[:, :, None] * picked, axis=1)).astype(jnp.bfloat16)
    return (layer_out, picked, gate_pre, up_pre)


def backward_layer(
    layer_in,
    upstream,
    picks,
    gain_row,
    router_w,
    gate_w,
    up_w,
    down_w,
    picked,
    gate_pre,
    up_pre,
    experts,
    capacity,
):
    values, inv_rms, hidden = norm_rows(layer_in, gain_row)
    gate_prob = gate_probs(hidden, router_w, picks)
    placing = slot_table(picks, experts, capacity)
    grad_out = upstream.astype(jnp.float32)
    d_prob = jnp.sum(grad_out[:, None, :] * picked, axis=2)
    d_gap = gate_prob[:, 0] * gate_prob[:, 1] * (d_prob[:, 0] - d_prob[:, 1])
    d_chosen = jnp.stack([d_gap, -d_gap], axis=1)
    expert_hot = (picks[:, :, None] == jnp.arange(experts, dtype=jnp.int32)[None, None, :]).astype(
        jnp.float32
    )
    d_logits = jnp.sum(d_chosen[:, :, None] * expert_hot, axis=1)
    scaled = (gate_prob[:, :, None] * grad_out[:, None, :]).astype(jnp.bfloat16)
    scaled = scaled.reshape(-1, grad_out.shape[1])
    arrived = deliver(send_rows(placing, scaled), experts, capacity)
    contract_last = (((1,), (1,)), ((), ()))
    d_active = lax.dot_general(arrived, down_w, contract_last, preferred_element_type=jnp.float32)
    gate_sig = jax.nn.sigmoid(gate_pre)
    d_gate = (d_active * up_pre * gate_sig * (1.0 + gate_pre * (1.0 - gate_sig))).astype(
        jnp.bfloat16
    )
    d_up = (d_active * gate_pre * gate_sig).astype(jnp.bfloat16)
    d_rows = lax.dot_general(d_gate, gate_w, contract_last, preferred_element_type=jnp.float32)
    d_rows = d_rows + lax.dot_general(d_up, up_w, contract_last, preferred_element_type=jnp.float32)
    summed = collect(d_rows.astype(jnp.bfloat16), experts, capacity)
    returned = jnp.dot(placing.astype(jnp.float32), summed, precision=lax.Precision.HIGHEST)
    returned = returned.reshape(layer_in.shape[0], picks.shape[1], -1)
    d_hidden = jnp.sum(returned, axis=1) + jnp.dot(
        d_logits, router_w.astype(jnp.float32).T, precision=lax.Precision.HIGHEST
    )
    router_term = jnp.dot(hidden.astype(jnp.float32).T, d_logits, precision=lax.Precision.HIGHEST)
    weighted = gain_row * d_hidden
    cubed = inv_rms * inv_rms * inv_rms
    d_in = (
        grad_out
        + inv_rms * weighted
        - values * cubed * jnp.mean(values * weighted, axis=-1, keepdims=True)
    )
    return (d_in.astype(jnp.bfloat16), router_term)


def fetch_micro(stored, which_mb):
    return lax.dynamic_index_in_dim(stored, which_mb, 0, keepdims=False)


def store_micro(stored, fresh, which_mb, in_range):
    previous = lax.dynamic_index_in_dim(stored, which_mb, 0, keepdims=False)
    return lax.dynamic_update_index_in_dim(
        stored, jnp.where(in_range, fresh, previous), which_mb, 0
    )


def per_device(inputs, cotangent, norm_gain, router, w_gate, w_up, w_down, routes):
    section_count = lax.axis_size("section")
    section_id = lax.axis_index("section")
    micro_count, tok_rows, model_width = inputs.shape
    experts = router.shape[2]
    top_k = routes.shape[3]
    capacity = 3 * top_k * tok_rows // (2 * experts)
    gate_w = w_gate[0, 0]
    up_w = w_up[0, 0]
    down_w = w_down[0, 0]
    gain_row = norm_gain[0].astype(jnp.float32)
    router_w = router[0]
    picks_all = routes[0]
    expert_rows = experts * lax.axis_size("dp") * capacity
    hidden_units = gate_w.shape[1]
    tick_count = micro_count + section_count - 1
    carried = jnp.zeros((tok_rows, model_width), jnp.bfloat16)
    outputs_all = jnp.zeros((micro_count, tok_rows, model_width), jnp.bfloat16)
    stash_in = jnp.zeros((micro_count, tok_rows, model_width), jnp.bfloat16)
    stash_pick = jnp.zeros((micro_count, tok_rows, top_k, model_width), jnp.float32)
    stash_gate = jnp.zeros((micro_count, expert_rows, hidden_units), jnp.float32)
    stash_up = jnp.zeros((micro_count, expert_rows, hidden_units), jnp.float32)
    for moment in range(tick_count):
        position = moment - section_id
        in_range = (position >= 0) & (position < micro_count)
        which_mb = jnp.clip(position, 0, micro_count - 1)
        layer_in = jnp.where(section_id == 0, fetch_micro(inputs, which_mb), carried)
        picks = fetch_micro(picks_all, which_mb)
        layer_out, picked, gate_pre, up_pre = forward_layer(
            layer_in, picks, gain_row, router_w, gate_w, up_w, down_w, experts, capacity
        )
        outputs_all = store_micro(outputs_all, layer_out, which_mb, in_range)
        stash_in = store_micro(stash_in, layer_in, which_mb, in_range)
        stash_pick = store_micro(stash_pick, picked, which_mb, in_range)
        stash_gate = store_micro(stash_gate, gate_pre, which_mb, in_range)
        stash_up = store_micro(stash_up, up_pre, which_mb, in_range)
        if moment + 1 < tick_count:
            carried = passed_along(layer_out, "section", 1)
    carried = jnp.zeros((tok_rows, model_width), jnp.bfloat16)
    grads_all = jnp.zeros((micro_count, tok_rows, model_width), jnp.bfloat16)
    router_sum = jnp.zeros((model_width, experts), jnp.float32)
    for moment in range(tick_count):
        position = moment - (section_count - 1 - section_id)
        in_range = (position >= 0) & (position < micro_count)
        which_mb = jnp.clip(position, 0, micro_count - 1)
        upstream = jnp.where(
            section_id == section_count - 1, fetch_micro(cotangent, which_mb), carried
        )
        d_in, router_term = backward_layer(
            fetch_micro(stash_in, which_mb),
            upstream,
            fetch_micro(picks_all, which_mb),
            gain_row,
            router_w,
            gate_w,
            up_w,
            down_w,
            fetch_micro(stash_pick, which_mb),
            fetch_micro(stash_gate, which_mb),
            fetch_micro(stash_up, which_mb),
            experts,
            capacity,
        )
        grads_all = store_micro(grads_all, d_in, which_mb, in_range)
        router_sum = router_sum + jnp.where(in_range, router_term, 0.0)
        if moment + 1 < tick_count:
            carried = passed_along(d_in, "section", -1)
    router_total = lax.psum(router_sum, ("expert", "dp"))
    return (outputs_all[None], grads_all[None], router_total[None])


def solution(mesh):
    placed = (
        P(None, ("expert", "dp"), None),
        P(None, ("expert", "dp"), None),
        P("section", None),
        P("section", None, None),
        P("section", "expert", None, "dp"),
        P("section", "expert", None, "dp"),
        P("section", "expert", "dp", None),
        P("section", None, ("expert", "dp"), None),
    )
    return jax.shard_map(
        per_device,
        mesh=mesh,
        in_specs=placed,
        out_specs=(
            P("section", None, ("expert", "dp"), None),
            P("section", None, ("expert", "dp"), None),
            P("section", None, None),
        ),
        check_vma=False,
    )
```

profile of v0, /device:TPU:0, one launch (start us, length us, event | category | flops | bytes accessed | tf_op | source)
XLA Modules:
  0.0 985.6 jit_solution(17254181758903616295)
XLA Ops:
  13.8 9.5 all-to-all-start
  30.7 16.1 %all-to-all-done = bf16[64,3,3072]{2,1,0:T(4,128)(2,1)S(1)} async-done(((bf16[64,3,3072]{2,1,0:T(4,128)(2,1)}), bf16[64,3,3072]{2,1,0:T(4,128)(2,1)S(1)}, u32[]{:S(2)}, u32[]{:S(2)}) %all-to-all-start) | async-done | bytes 1179680 | tf_op jit(solution)/shard_map/all_to_all | solution.py:41
  48.9 4.8 bitcast_dynamic-update-slice_fusion.5
  59.2 2.1 reshape.574
  61.3 5.1 all-to-all-start.1
  71.7 18.2 %all-to-all-done.1 = bf16[64,3,3072]{2,1,0:T(4,128)(2,1)S(1)} async-done(((bf16[64,3,3072]{2,1,0:T(4,128)(2,1)}), bf16[64,3,3072]{2,1,0:T(4,128)(2,1)S(1)}, u32[]{:S(2)}, u32[]{:S(2)}) %all-to-all-start.1) | async-done | bytes 1179680 | tf_op jit(solution)/shard_map/all_to_all | solution.py:48
  92.8 5.4 collective-permute-start
  98.2 2.5 constant_dynamic-slice_fusion.9
  104.4 5.7 all-to-all-start.2
  113.1 20.3 %all-to-all-done.2 = bf16[64,3,3072]{2,1,0:T(4,128)(2,1)} async-done(((bf16[64,3,3072]{2,1,0:T(4,128)(2,1)}), bf16[64,3,3072]{2,1,0:T(4,128)(2,1)}, u32[]{:S(2)}, u32[]{:S(2)}) %all-to-all-start.2) | async-done | bytes 1179680 | tf_op jit(solution)/shard_map/all_to_all | solution.py:41
  133.4 2.9 reshape.579
  136.4 5.4 bitcast_dynamic-update-slice_fusion.4
  148.0 5.1 all-to-all-start.3
  155.6 20.9 %all-to-all-done.3 = bf16[64,3,3072]{2,1,0:T(4,128)(2,1)S(1)} async-done(((bf16[64,3,3072]{2,1,0:T(4,128)(2,1)}), bf16[64,3,3072]{2,1,0:T(4,128)(2,1)S(1)}, u32[]{:S(2)}, u32[]{:S(2)}) %all-to-all-start.3) | async-done | bytes 1179680 | tf_op jit(solution)/shard_map/all_to_all | solution.py:48
  180.3 4.9 collective-permute-start.1
  189.5 6.0 all-to-all-start.4
  197.9 20.9 %all-to-all-done.4 = bf16[64,3,3072]{2,1,0:T(4,128)(2,1)} async-done(((bf16[64,3,3072]{2,1,0:T(4,128)(2,1)}), bf16[64,3,3072]{2,1,0:T(4,128)(2,1)}, u32[]{:S(2)}, u32[]{:S(2)}) %all-to-all-start.4) | async-done | bytes 1179680 | tf_op jit(solution)/shard_map/all_to_all | solution.py:41
  218.8 2.9 reshape.585
  221.8 5.4 bitcast_dynamic-update-slice_fusion.3
  233.4 4.9 all-to-all-start.5
  240.3 21.5 %all-to-all-done.5 = bf16[64,3,3072]{2,1,0:T(4,128)(2,1)S(1)} async-done(((bf16[64,3,3072]{2,1,0:T(4,128)(2,1)}), bf16[64,3,3072]{2,1,0:T(4,128)(2,1)S(1)}, u32[]{:S(2)}, u32[]{:S(2)}) %all-to-all-start.5) | async-done | bytes 1179680 | tf_op jit(solution)/shard_map/all_to_all | solution.py:48
  267.0 5.8 all-to-all-start.6
  275.1 21.1 %all-to-all-done.6 = bf16[64,3,3072]{2,1,0:T(4,128)(2,1)} async-done(((bf16[64,3,3072]{2,1,0:T(4,128)(2,1)}), bf16[64,3,3072]{2,1,0:T(4,128)(2,1)}, u32[]{:S(2)}, u32[]{:S(2)}) %all-to-all-start.6) | async-done | bytes 1179680 | tf_op jit(solution)/shard_map/all_to_all | solution.py:41
  296.2 2.8 reshape.591
  299.0 5.1 fusion.4
  304.2 3.5 fusion.16
  307.8 2.4 fusion.60
  312.3 5.0 all-to-all-start.7
  318.1 22.5 %all-to-all-done.7 = bf16[64,3,3072]{2,1,0:T(4,128)(2,1)S(1)} async-done(((bf16[64,3,3072]{2,1,0:T(4,128)(2,1)}), bf16[64,3,3072]{2,1,0:T(4,128)(2,1)S(1)}, u32[]{:S(2)}, u32[]{:S(2)}) %all-to-all-start.7) | async-done | bytes 1179680 | tf_op jit(solution)/shard_map/all_to_all | solution.py:48
  344.5 5.2 collective-permute-done.2
  352.6 5.8 all-to-all-start.8
  359.3 22.4 %all-to-all-done.8 = bf16[64,3,3072]{2,1,0:T(4,128)(2,1)} async-done(((bf16[64,3,3072]{2,1,0:T(4,128)(2,1)}), bf16[64,3,3072]{2,1,0:T(4,128)(2,1)}, u32[]{:S(2)}, u32[]{:S(2)}) %all-to-all-start.8) | async-done | bytes 1179680 | tf_op jit(solution)/shard_map/all_to_all | solution.py:41
  381.8 4.0 reshape.597
  385.7 5.5 fusion.2
  391.3 3.5 fusion.14
  394.9 2.4 fusion.57
  399.3 4.9 all-to-all-start.9
  405.5 22.2 %all-to-all-done.9 = bf16[64,3,3072]{2,1,0:T(4,128)(2,1)S(1)} async-done(((bf16[64,3,3072]{2,1,0:T(4,128)(2,1)}), bf16[64,3,3072]{2,1,0:T(4,128)(2,1)S(1)}, u32[]{:S(2)}, u32[]{:S(2)}) %all-to-all-start.9) | async-done | bytes 1179680 | tf_op jit(solution)/shard_map/all_to_all | solution.py:48
  430.6 6.2 collective-permute-done.3
  439.6 5.9 all-to-all-start.10
  446.0 22.9 %all-to-all-done.10 = bf16[64,3,3072]{2,1,0:T(4,128)(2,1)} async-done(((bf16[64,3,3072]{2,1,0:T(4,128)(2,1)}), bf16[64,3,3072]{2,1,0:T(4,128)(2,1)}, u32[]{:S(2)}, u32[]{:S(2)}) %all-to-all-start.10) | async-done | bytes 1179680 | tf_op jit(solution)/shard_map/all_to_all | solution.py:41
  468.8 4.0 reshape.603
  472.8 5.5 fusion
  478.4 3.5 fusion.12
  481.9 2.4 fusion.54
  486.4 5.1 all-to-all-start.11
  493.0 21.9 %all-to-all-done.11 = bf16[64,3,3072]{2,1,0:T(4,128)(2,1)S(1)} async-done(((bf16[64,3,3072]{2,1,0:T(4,128)(2,1)}), bf16[64,3,3072]{2,1,0:T(4,128)(2,1)S(1)}, u32[]{:S(2)}, u32[]{:S(2)}) %all-to-all-start.11) | async-done | bytes 1179680 | tf_op jit(solution)/shard_map/all_to_all | solution.py:48
  516.5 460.3 %all-reduce.2.cloned.1.call-done = f32[1,3072,8]{1,2,0:T(8,128)} async-done(((f32[1,3072,8]{1,2,0:T(8,128)}), f32[1,3072,8]{1,2,0:T(8,128)}) %all-reduce.2.cloned.1.call-update) | async-done | bytes 98320 | tf_op jit(solution)/shard_map/psum | solution.py:222
  (468 shorter events, 96.7 us)
Async XLA Ops:
  7.2 16.3 %copy-start = (bf16[1,3072,8]{1,2,0:T(8,128)(2,1)S(1)}, bf16[1,3072,8]{1,2,0:T(8,128)(2,1)}, u32[]{:S(2)}) copy-start(bf16[1,3072,8]{1,2,0:T(8,128)(2,1)} %param.13) | copy-start | bytes 147460
  11.3 16.8 %copy-start.46 = (s32[1,1,8,2]{2,3,1,0:T(2,128)}, s32[1,1,8,2]{2,3,1,0:T(2,128)S(1)}, u32[]{:S(2)}) copy-start(s32[1,1,8,2]{2,3,1,0:T(2,128)S(1)} %get-tuple-element.40) | copy-start | bytes 196
  13.8 9.6 copy-start.21
  13.8 33.0 %all-to-all-start = ((bf16[64,3,3072]{2,1,0:T(4,128)(2,1)}), bf16[64,3,3072]{2,1,0:T(4,128)(2,1)S(1)}, u32[]{:S(2)}, u32[]{:S(2)}) async-start(bf16[64,3,3072]{2,1,0:T(4,128)(2,1)} %bitcast.7), calls=%async_computation | async-start | bytes 3145728 | tf_op jit(solution)/shard_map/all_to_all | solution.py:41
  29.0 19.1 %copy-start.61 = (s32[16]{0:T(128)}, s32[16]{0:T(128)S(1)}, u32[]{:S(2)}) copy-start(s32[16]{0:T(128)S(1)} %get-tuple-element.74) | copy-start | bytes 196
  30.7 36.4 %copy-start.24 = (f32[8,3072]{1,0:T(8,128)}, f32[8,3072]{1,0:T(8,128)S(1)}, u32[]{:S(2)}) copy-start(f32[8,3072]{1,0:T(8,128)S(1)} %bitcast_convert_fusion) | copy-start | bytes 294916
  57.0 41.2 %copy-start.1 = (f32[2,192,1024]{2,1,0:T(8,128)}, f32[2,192,1024]{2,1,0:T(8,128)S(1)}, u32[]{:S(2)}) copy-start(f32[2,192,1024]{2,1,0:T(8,128)S(1)} %get-tuple-element.57) | copy-start | bytes 4718596
  61.3 28.5 %all-to-all-start.1 = ((bf16[64,3,3072]{2,1,0:T(4,128)(2,1)}), bf16[64,3,3072]{2,1,0:T(4,128)(2,1)S(1)}, u32[]{:S(2)}, u32[]{:S(2)}) async-start(bf16[64,3,3072]{2,1,0:T(4,128)(2,1)} %reshape.574), calls=%async_computation.1 | async-start | bytes 3145728 | tf_op jit(solution)/shard_map/all_to_all | solution.py:48
  69.6 22.8 %copy-start.54 = (s32[8,2]{0,1:T(2,128)S(1)}, s32[8,2]{0,1:T(2,128)}, u32[]{:S(2)}) copy-start(s32[8,2]{0,1:T(2,128)} %multiply_add_fusion.5) | copy-start | bytes 196
  92.8 8.0 collective-permute-start
  104.4 29.0 %all-to-all-start.2 = ((bf16[64,3,3072]{2,1,0:T(4,128)(2,1)}), bf16[64,3,3072]{2,1,0:T(4,128)(2,1)}, u32[]{:S(2)}, u32[]{:S(2)}) async-start(bf16[64,3,3072]{2,1,0:T(4,128)(2,1)} %bitcast.17), calls=%async_computation.2 | async-start | bytes 3145728 | tf_op jit(solution)/shard_map/all_to_all | solution.py:41
  133.4 8.4 slice-start.8
  136.4 8.1 slice-start.20
  148.0 28.5 %all-to-all-start.3 = ((bf16[64,3,3072]{2,1,0:T(4,128)(2,1)}), bf16[64,3,3072]{2,1,0:T(4,128)(2,1)S(1)}, u32[]{:S(2)}, u32[]{:S(2)}) async-start(bf16[64,3,3072]{2,1,0:T(4,128)(2,1)} %reshape.580), calls=%async_computation.3 | async-start | bytes 3145728 | tf_op jit(solution)/shard_map/all_to_all | solution.py:48
  155.6 23.6 %copy-start.53 = (s32[8,2]{0,1:T(2,128)S(1)}, s32[8,2]{0,1:T(2,128)}, u32[]{:S(2)}) copy-start(s32[8,2]{0,1:T(2,128)} %multiply_add_fusion.4) | copy-start | bytes 196
  155.6 29.7 %copy-start.4 = (f32[2,192,1024]{2,1,0:T(8,128)S(1)}, f32[2,192,1024]{2,1,0:T(8,128)}, u32[]{:S(2)}) copy-start(f32[2,192,1024]{2,1,0:T(8,128)} %copy-done.3) | copy-start | bytes 4718596
  178.0 9.0 copy-start.41
  179.1 8.2 copy-start.68
  180.3 17.5 %copy-start.28 = (bf16[2,8,3072]{2,1,0:T(8,128)(2,1)}, bf16[2,8,3072]{2,1,0:T(8,128)(2,1)S(1)}, u32[]{:S(2)}) copy-start(bf16[2,8,3072]{2,1,0:T(8,128)(2,1)S(1)} %get-tuple-element.27) | copy-start | bytes 294916
  180.3 6.7 collective-permute-start.1
  189.5 29.4 %all-to-all-start.4 = ((bf16[64,3,3072]{2,1,0:T(4,128)(2,1)}), bf16[64,3,3072]{2,1,0:T(4,128)(2,1)}, u32[]{:S(2)}, u32[]{:S(2)}) async-start(bf16[64,3,3072]{2,1,0:T(4,128)(2,1)} %bitcast.26), calls=%async_computation.4 | async-start | bytes 3145728 | tf_op jit(solution)/shard_map/all_to_all | solution.py:41
  218.8 8.4 slice-start.10
  221.8 8.1 slice-start.22
  233.4 28.4 %all-to-all-start.5 = ((bf16[64,3,3072]{2,1,0:T(4,128)(2,1)}), bf16[64,3,3072]{2,1,0:T(4,128)(2,1)S(1)}, u32[]{:S(2)}, u32[]{:S(2)}) async-start(bf16[64,3,3072]{2,1,0:T(4,128)(2,1)} %reshape.586), calls=%async_computation.5 | async-start | bytes 3145728 | tf_op jit(solution)/shard_map/all_to_all | solution.py:48
  240.2 22.5 %copy-start.52 = (s32[8,2]{0,1:T(2,128)S(1)}, s32[8,2]{0,1:T(2,128)}, u32[]{:S(2)}) copy-start(s32[8,2]{0,1:T(2,128)} %multiply_add_fusion.3) | copy-start | bytes 196
  240.3 22.7 %copy-start.18 = (f32[2,8,2,3072]{3,1,2,0:T(8,128)S(1)}, f32[2,8,2,3072]{3,1,2,0:T(8,128)}, u32[]{:S(2)}) copy-start(f32[2,8,2,3072]{3,1,2,0:T(8,128)} %copy-done.17) | copy-start | bytes 1179652
  240.3 22.7 %copy-start.35 = (f32[1,8,2,3072]{3,1,2,0:T(8,128)S(1)}, f32[1,8,2,3072]{3,1,2,0:T(8,128)}, u32[]{:S(2)}) copy-start(f32[1,8,2,3072]{3,1,2,0:T(8,128)} %constant_dynamic-slice_fusion.6) | copy-start | bytes 589828
  267.0 37.1 %slice-start = ((s8[6291456]{0:T(1024)(128)(4,1)}), s8[2097152]{0:T(1024)(128)(4,1)S(1)}, s32[]{:S(2)}) async-start(s8[6291456]{0:T(1024)(128)(4,1)} %bitcast.549), calls=%async_computation.13 | async-start | bytes 4194304
  267.0 29.1 %all-to-all-start.6 = ((bf16[64,3,3072]{2,1,0:T(4,128)(2,1)}), bf16[64,3,3072]{2,1,0:T(4,128)(2,1)}, u32[]{:S(2)}, u32[]{:S(2)}) async-start(bf16[64,3,3072]{2,1,0:T(4,128)(2,1)} %bitcast.569), calls=%async_computation.6 | async-start | bytes 3145728 | tf_op jit(solution)/shard_map/all_to_all | solution.py:41
  299.0 8.8 slice-start.12
  312.3 28.4 %all-to-all-start.7 = ((bf16[64,3,3072]{2,1,0:T(4,128)(2,1)}), bf16[64,3,3072]{2,1,0:T(4,128)(2,1)S(1)}, u32[]{:S(2)}, u32[]{:S(2)}) async-start(bf16[64,3,3072]{2,1,0:T(4,128)(2,1)} %reshape.592), calls=%async_computation.7 | async-start | bytes 3145728 | tf_op jit(solution)/shard_map/all_to_all | solution.py:48
  318.1 24.0 %copy-start.39 = (bf16[2,8,3072]{2,1,0:T(8,128)(2,1)S(1)}, bf16[2,8,3072]{2,1,0:T(8,128)(2,1)}, u32[]{:S(2)}) copy-start(bf16[2,8,3072]{2,1,0:T(8,128)(2,1)} %param.11) | copy-start | bytes 294916
  318.1 24.0 %copy-start.59 = (f32[8]{0:T(128)S(1)}, f32[8]{0:T(128)}, u32[]{:S(2)}) copy-start(f32[8]{0:T(128)} %copy-done.58) | copy-start | bytes 100
  318.1 24.0 %copy-start.70 = (f32[8]{0:T(128)S(1)}, f32[8]{0:T(128)}, u32[]{:S(2)}) copy-start(f32[8]{0:T(128)} %get-tuple-element.49) | copy-start | bytes 100
  342.3 7.5 collective-permute-start.2
  352.6 38.6 %slice-start.2 = ((s8[6291456]{0:T(1024)(128)(4,1)}), s8[2097152]{0:T(1024)(128)(4,1)S(1)}, s32[]{:S(2)}) async-start(s8[6291456]{0:T(1024)(128)(4,1)} %bitcast.551), calls=%async_computation.15 | async-start | bytes 4194304
  352.6 29.2 %all-to-all-start.8 = ((bf16[64,3,3072]{2,1,0:T(4,128)(2,1)}), bf16[64,3,3072]{2,1,0:T(4,128)(2,1)}, u32[]{:S(2)}, u32[]{:S(2)}) async-start(bf16[64,3,3072]{2,1,0:T(4,128)(2,1)} %bitcast.567), calls=%async_computation.8 | async-start | bytes 3145728 | tf_op jit(solution)/shard_map/all_to_all | solution.py:41
  385.7 9.1 slice-start.14
  399.3 28.4 %all-to-all-start.9 = ((bf16[64,3,3072]{2,1,0:T(4,128)(2,1)}), bf16[64,3,3072]{2,1,0:T(4,128)(2,1)S(1)}, u32[]{:S(2)}, u32[]{:S(2)}) async-start(bf16[64,3,3072]{2,1,0:T(4,128)(2,1)} %reshape.598), calls=%async_computation.9 | async-start | bytes 3145728 | tf_op jit(solution)/shard_map/all_to_all | solution.py:48
  428.4 8.6 copy-start.31
  429.3 7.5 collective-permute-start.3
  439.6 38.7 %slice-start.4 = ((s8[6291456]{0:T(1024)(128)(4,1)}), s8[2097152]{0:T(1024)(128)(4,1)S(1)}, s32[]{:S(2)}) async-start(s8[6291456]{0:T(1024)(128)(4,1)} %bitcast.553), calls=%async_computation.17 | async-start | bytes 4194304
  439.6 29.2 %all-to-all-start.10 = ((bf16[64,3,3072]{2,1,0:T(4,128)(2,1)}), bf16[64,3,3072]{2,1,0:T(4,128)(2,1)}, u32[]{:S(2)}, u32[]{:S(2)}) async-start(bf16[64,3,3072]{2,1,0:T(4,128)(2,1)} %bitcast.568), calls=%async_computation.10 | async-start | bytes 3145728 | tf_op jit(solution)/shard_map/all_to_all | solution.py:41
  472.8 9.1 slice-start.16
  486.4 28.5 %all-to-all-start.11 = ((bf16[64,3,3072]{2,1,0:T(4,128)(2,1)}), bf16[64,3,3072]{2,1,0:T(4,128)(2,1)S(1)}, u32[]{:S(2)}, u32[]{:S(2)}) async-start(bf16[64,3,3072]{2,1,0:T(4,128)(2,1)} %reshape.604), calls=%async_computation.11 | async-start | bytes 3145728 | tf_op jit(solution)/shard_map/all_to_all | solution.py:48
  491.5 485.3 %all-reduce.2.cloned.1.call-start = ((), (), s32[]{:S(2)}) async-start(), calls=%async_computation.12 | async-start | bytes 196608 | tf_op jit(solution)/shard_map/psum | solution.py:222
  491.6 24.2 %copy-start.43 = (bf16[1,2,8,3072]{3,2,1,0:T(8,128)(2,1)}, bf16[1,2,8,3072]{3,2,1,0:T(8,128)(2,1)S(1)}, u32[]{:S(2)}) copy-start(bf16[1,2,8,3072]{3,2,1,0:T(8,128)(2,1)S(1)} %fusion.176) | copy-start | bytes 294916
  516.5 461.8 %copy-start.42 = (bf16[1,2,8,3072]{3,2,1,0:T(8,128)(2,1)}, bf16[1,2,8,3072]{3,2,1,0:T(8,128)(2,1)S(1)}, u32[]{:S(2)}) copy-start(bf16[1,2,8,3072]{3,2,1,0:T(8,128)(2,1)S(1)} %fusion.188) | copy-start | bytes 294916
  (64 other events, 263.9 us)
Sparse Core Ops, SparseCore 0:
  495.3 481.3 all-reduce.1
where the time goes:
time: 996 us; the launch traced here: 986 us
  waiting for transfers between devices  723 us (73%)
  starting transfers between devices  81.9 us (8%)
  local copies, waits for them, and re-layouts  79.4 us (8%)
  matrix products  65.2 us (7%)
  other arithmetic  19.5 us (2%)
  between operations  16.4 us (2%)
    psum x1, waiting for transfers between devices, per_device(): router_total = lax.psum(router_sum, ('expert', 'dp'))  460 us
    all_to_all x6, waiting for transfers between devices, collect(): lax.all_to_all(partial_out.reshape(experts * replicas, capacity, model_wi...  127 us
    all_to_all x6, waiting for transfers between devices, deliver(): lax.all_to_all(tiled, ('expert', 'dp'), split_axis=0, concat_axis=0, tile...  124 us
    all_to_all x6, starting transfers between devices, deliver(): lax.all_to_all(tiled, ('expert', 'dp'), split_axis=0, concat_axis=0, tile...  38.8 us
    all_to_all x6, starting transfers between devices, collect(): lax.all_to_all(partial_out.reshape(experts * replicas, capacity, model_wi...  30.1 us
  transfers between devices with their start and end apart: 17, of which 16 were waited for; matrix products, arithmetic and copies ran while one was open for 3% of the time, Pallas kernels for 0%

commit v1 on v0

--- a/solution.py
+++ b/solution.py
@@ -219,7 +219,7 @@
         router_sum = router_sum + jnp.where(in_range, router_term, 0.0)
         if moment + 1 < tick_count:
             carried = passed_along(d_in, "section", -1)
-    router_total = lax.psum(router_sum, ("expert", "dp"))
+    router_total = jnp.sum(lax.all_gather(router_sum, ("expert", "dp")), axis=0)
     return (outputs_all[None], grads_all[None], router_total[None])
 
 

time: 996 us -> 588 us (0.59)
  waiting for transfers between devices: 723 us -> 290 us
  blocking collectives: 0 us -> 32.3 us
    psum x1 -> x0, waiting for transfers between devices: 460 us -> none  [per_device(): router_total = lax.psum(router_sum, ('expert', 'dp'))]
    all_gather x0 -> x1, waiting for transfers between devices: none -> 42.6 us  [per_device(): router_total = jnp.sum(lax.all_gather(router_sum, ('expert', 'dp')), axis=0)]
    all_to_all x0 -> x1, blocking collectives: none -> 32.3 us  [deliver(): lax.all_to_all(tiled, ('expert', 'dp'), split_axis=0, concat_axis=0, tile...]
    all_to_all x6 -> x5, waiting for transfers between devices: 124 us -> 103 us  [deliver(): lax.all_to_all(tiled, ('expert', 'dp'), split_axis=0, concat_axis=0, tile...]
    all_to_all x6 -> x5, starting transfers between devices: 38.8 us -> 33 us  [deliver(): lax.all_to_all(tiled, ('expert', 'dp'), split_axis=0, concat_axis=0, tile...]
  transfers between devices with their start and end apart: 17 -> 16, of which waited for: 16 -> 15; matrix products, arithmetic and copies ran while one was open for 3% -> 8% of each run, Pallas kernels for 0% -> 0%
where the time goes in v1:
time: 588 us; the launch traced here: 577 us
  waiting for transfers between devices  290 us (49%)
  starting transfers between devices  76.5 us (13%)
  local copies, waits for them, and re-layouts  75.5 us (13%)
  matrix products  65.1 us (11%)
  blocking collectives  32.3 us (5%)
  other arithmetic  21.9 us (4%)
  between operations  16.3 us (3%)
    all_to_all x6, waiting for transfers between devices, collect(): lax.all_to_all(partial_out.reshape(experts * replicas, capacity, model_wi...  132 us
    all_to_all x5, waiting for transfers between devices, deliver(): lax.all_to_all(tiled, ('expert', 'dp'), split_axis=0, concat_axis=0, tile...  103 us
    all_gather x1, waiting for transfers between devices, per_device(): router_total = jnp.sum(lax.all_gather(router_sum, ('expert', 'dp')), axis=0)  42.6 us
    all_to_all x5, starting transfers between devices, deliver(): lax.all_to_all(tiled, ('expert', 'dp'), split_axis=0, concat_axis=0, tile...  33 us
    all_to_all x1, blocking collectives, deliver(): lax.all_to_all(tiled, ('expert', 'dp'), split_axis=0, concat_axis=0, tile...  32.3 us
    all_to_all x6, starting transfers between devices, collect(): lax.all_to_all(partial_out.reshape(experts * replicas, capacity, model_wi...  30.3 us
    reshape x6, local copies, waits for them, and re-layouts, deliver(): return arrived.reshape(-1, model_width)  17.6 us
    dot_general x3, matrix products, backward_layer(): lax.dot_general(arrived, down_w, contract_last, preferred_element_type=jn...  16.2 us
  transfers between devices with their start and end apart: 16, of which 15 were waited for; matrix products, arithmetic and copies ran while one was open for 8% of the time, Pallas kernels for 0%

profile of v1, /device:TPU:0, one launch (start us, length us, event | category | flops | bytes accessed | tf_op | source)
XLA Modules:
  0.0 577.1 jit_solution(6347327815988128766)
XLA Ops:
  13.8 9.5 %all-to-all-start = ((bf16[64,3,3072]{2,1,0:T(4,128)(2,1)}), bf16[64,3,3072]{2,1,0:T(4,128)(2,1)S(1)}, u32[]{:S(2)}, u32[]{:S(2)}) async-start(bf16[64,3,3072]{2,1,0:T(4,128)(2,1)} %bitcast.7), calls=%async_computation | async-start | bytes 3145728 | tf_op jit(solution)/shard_map/all_to_all | solution.py:41
  28.5 18.3 %all-to-all-done = bf16[64,3,3072]{2,1,0:T(4,128)(2,1)S(1)} async-done(((bf16[64,3,3072]{2,1,0:T(4,128)(2,1)}), bf16[64,3,3072]{2,1,0:T(4,128)(2,1)S(1)}, u32[]{:S(2)}, u32[]{:S(2)}) %all-to-all-start) | async-done | bytes 1179680 | tf_op jit(solution)/shard_map/all_to_all | solution.py:41
  48.9 4.8 bitcast_dynamic-update-slice_fusion.5
  61.3 5.0 all-to-all-start.1
  71.3 18.4 %all-to-all-done.1 = bf16[64,3,3072]{2,1,0:T(4,128)(2,1)S(1)} async-done(((bf16[64,3,3072]{2,1,0:T(4,128)(2,1)}), bf16[64,3,3072]{2,1,0:T(4,128)(2,1)S(1)}, u32[]{:S(2)}, u32[]{:S(2)}) %all-to-all-start.1) | async-done | bytes 1179680 | tf_op jit(solution)/shard_map/all_to_all | solution.py:48
  92.6 5.4 collective-permute-start
  98.1 2.4 constant_dynamic-slice_fusion.9
  104.1 5.7 all-to-all-start.2
  112.8 20.4 %all-to-all-done.2 = bf16[64,3,3072]{2,1,0:T(4,128)(2,1)} async-done(((bf16[64,3,3072]{2,1,0:T(4,128)(2,1)}), bf16[64,3,3072]{2,1,0:T(4,128)(2,1)}, u32[]{:S(2)}, u32[]{:S(2)}) %all-to-all-start.2) | async-done | bytes 1179680 | tf_op jit(solution)/shard_map/all_to_all | solution.py:41
  133.1 2.9 reshape.579
  136.1 5.4 bitcast_dynamic-update-slice_fusion.4
  147.7 5.1 all-to-all-start.3
  155.3 20.9 %all-to-all-done.3 = bf16[64,3,3072]{2,1,0:T(4,128)(2,1)S(1)} async-done(((bf16[64,3,3072]{2,1,0:T(4,128)(2,1)}), bf16[64,3,3072]{2,1,0:T(4,128)(2,1)S(1)}, u32[]{:S(2)}, u32[]{:S(2)}) %all-to-all-start.3) | async-done | bytes 1179680 | tf_op jit(solution)/shard_map/all_to_all | solution.py:48
  180.0 5.1 collective-permute-start.1
  189.3 6.1 %all-to-all-start.4 = ((bf16[64,3,3072]{2,1,0:T(4,128)(2,1)}), bf16[64,3,3072]{2,1,0:T(4,128)(2,1)}, u32[]{:S(2)}, u32[]{:S(2)}) async-start(bf16[64,3,3072]{2,1,0:T(4,128)(2,1)} %bitcast.26), calls=%async_computation.4 | async-start | bytes 3145728 | tf_op jit(solution)/shard_map/all_to_all | solution.py:41
  197.7 20.9 %all-to-all-done.4 = bf16[64,3,3072]{2,1,0:T(4,128)(2,1)} async-done(((bf16[64,3,3072]{2,1,0:T(4,128)(2,1)}), bf16[64,3,3072]{2,1,0:T(4,128)(2,1)}, u32[]{:S(2)}, u32[]{:S(2)}) %all-to-all-start.4) | async-done | bytes 1179680 | tf_op jit(solution)/shard_map/all_to_all | solution.py:41
  218.6 2.9 reshape.585
  221.6 5.4 bitcast_dynamic-update-slice_fusion.3
  231.1 2.1 reshape.586
  233.2 4.9 all-to-all-start.5
  240.4 21.2 %all-to-all-done.5 = bf16[64,3,3072]{2,1,0:T(4,128)(2,1)S(1)} async-done(((bf16[64,3,3072]{2,1,0:T(4,128)(2,1)}), bf16[64,3,3072]{2,1,0:T(4,128)(2,1)S(1)}, u32[]{:S(2)}, u32[]{:S(2)}) %all-to-all-start.5) | async-done | bytes 1179680 | tf_op jit(solution)/shard_map/all_to_all | solution.py:48
  266.8 5.8 %all-to-all-start.6 = ((bf16[64,3,3072]{2,1,0:T(4,128)(2,1)}), bf16[64,3,3072]{2,1,0:T(4,128)(2,1)}, u32[]{:S(2)}, u32[]{:S(2)}) async-start(bf16[64,3,3072]{2,1,0:T(4,128)(2,1)} %bitcast.568), calls=%async_computation.6 | async-start | bytes 3145728 | tf_op jit(solution)/shard_map/all_to_all | solution.py:41
  274.8 21.1 %all-to-all-done.6 = bf16[64,3,3072]{2,1,0:T(4,128)(2,1)} async-done(((bf16[64,3,3072]{2,1,0:T(4,128)(2,1)}), bf16[64,3,3072]{2,1,0:T(4,128)(2,1)}, u32[]{:S(2)}, u32[]{:S(2)}) %all-to-all-start.6) | async-done | bytes 1179680 | tf_op jit(solution)/shard_map/all_to_all | solution.py:41
  296.0 2.8 reshape.591
  298.8 5.2 fusion.4
  304.0 3.5 fusion.16
  307.6 2.4 fusion.60
  312.1 5.0 all-to-all-start.7
  317.9 22.5 %all-to-all-done.7 = bf16[64,3,3072]{2,1,0:T(4,128)(2,1)S(1)} async-done(((bf16[64,3,3072]{2,1,0:T(4,128)(2,1)}), bf16[64,3,3072]{2,1,0:T(4,128)(2,1)S(1)}, u32[]{:S(2)}, u32[]{:S(2)}) %all-to-all-start.7) | async-done | bytes 1179680 | tf_op jit(solution)/shard_map/all_to_all | solution.py:48
  344.3 5.2 collective-permute-done.2
  352.4 5.9 %all-to-all-start.8 = ((bf16[64,3,3072]{2,1,0:T(4,128)(2,1)}), bf16[64,3,3072]{2,1,0:T(4,128)(2,1)}, u32[]{:S(2)}, u32[]{:S(2)}) async-start(bf16[64,3,3072]{2,1,0:T(4,128)(2,1)} %bitcast.68), calls=%async_computation.8 | async-start | bytes 3145728 | tf_op jit(solution)/shard_map/all_to_all | solution.py:41
  358.9 22.6 %all-to-all-done.8 = bf16[64,3,3072]{2,1,0:T(4,128)(2,1)} async-done(((bf16[64,3,3072]{2,1,0:T(4,128)(2,1)}), bf16[64,3,3072]{2,1,0:T(4,128)(2,1)}, u32[]{:S(2)}, u32[]{:S(2)}) %all-to-all-start.8) | async-done | bytes 1179680 | tf_op jit(solution)/shard_map/all_to_all | solution.py:41
  381.5 3.9 reshape.597
  385.5 5.5 fusion.2
  391.0 3.5 fusion.14
  394.6 2.4 fusion.57
  399.1 4.9 all-to-all-start.9
  405.3 22.2 %all-to-all-done.9 = bf16[64,3,3072]{2,1,0:T(4,128)(2,1)S(1)} async-done(((bf16[64,3,3072]{2,1,0:T(4,128)(2,1)}), bf16[64,3,3072]{2,1,0:T(4,128)(2,1)S(1)}, u32[]{:S(2)}, u32[]{:S(2)}) %all-to-all-start.9) | async-done | bytes 1179680 | tf_op jit(solution)/shard_map/all_to_all | solution.py:48
  430.6 5.9 %collective-permute-done.3 = bf16[8,3072]{1,0:T(8,128)(2,1)S(1)} collective-permute-done((bf16[8,3072]{1,0:T(8,128)(2,1)S(1)}, bf16[8,3072]{1,0:T(8,128)(2,1)S(1)}, u32[]{:S(2)}, u32[]{:S(2)}) %collective-permute-start.3) | collective-permute-done | bytes 49184 | tf_op jit(solution)/shard_map/ppermute | solution.py:12
  439.8 32.3 %all_to_all.60 = bf16[64,3,3072]{2,1,0:T(4,128)(2,1)} all-to-all(bf16[64,3,3072]{2,1,0:T(4,128)(2,1)S(1)} %bitcast.569), channel_id=1, replica_groups=mesh['section'=2,'expert'=8,'dp'=8] {'expert','dp'}, dimensions={0} | all-to-all | bytes 2359296 | tf_op jit(solution)/shard_map/all_to_all | solution.py:41
  472.1 4.0 reshape.603
  476.1 5.5 fusion
  481.7 3.5 fusion.12
  485.3 2.4 fusion.54
  489.8 5.4 all-to-all-start.11
  495.5 26.4 %all-to-all-done.11 = bf16[64,3,3072]{2,1,0:T(4,128)(2,1)S(1)} async-done(((bf16[64,3,3072]{2,1,0:T(4,128)(2,1)}), bf16[64,3,3072]{2,1,0:T(4,128)(2,1)S(1)}, u32[]{:S(2)}, u32[]{:S(2)}) %all-to-all-start.11) | async-done | bytes 1179680 | tf_op jit(solution)/shard_map/all_to_all | solution.py:48
  523.5 42.6 %all-gather.3.cloned.1.call-done = f32[196608,8]{0,1:T(8,128)} async-done(((f32[3072,8]{0,1:T(8,128)}), f32[196608,8]{0,1:T(8,128)}) %all-gather.3.cloned.1.call-update) | async-done | bytes 6291472 | tf_op jit(solution)/shard_map/all_gather | solution.py:222
  566.1 3.7 reduce_sum.360
  (453 shorter events, 91.6 us)
Async XLA Ops:
  7.2 16.3 %copy-start = (bf16[1,3072,8]{1,2,0:T(8,128)(2,1)S(1)}, bf16[1,3072,8]{1,2,0:T(8,128)(2,1)}, u32[]{:S(2)}) copy-start(bf16[1,3072,8]{1,2,0:T(8,128)(2,1)} %param.13) | copy-start | bytes 147460
  11.3 15.1 %copy-start.46 = (s32[1,1,8,2]{2,3,1,0:T(2,128)}, s32[1,1,8,2]{2,3,1,0:T(2,128)S(1)}, u32[]{:S(2)}) copy-start(s32[1,1,8,2]{2,3,1,0:T(2,128)S(1)} %get-tuple-element.40) | copy-start | bytes 196
  13.8 9.6 %copy-start.21 = (bf16[2,8,3072]{2,1,0:T(8,128)(2,1)S(1)}, bf16[2,8,3072]{2,1,0:T(8,128)(2,1)}, u32[]{:S(2)}) copy-start(bf16[2,8,3072]{2,1,0:T(8,128)(2,1)} %param.10) | copy-start | bytes 294916
  13.8 33.0 %all-to-all-start = ((bf16[64,3,3072]{2,1,0:T(4,128)(2,1)}), bf16[64,3,3072]{2,1,0:T(4,128)(2,1)S(1)}, u32[]{:S(2)}, u32[]{:S(2)}) async-start(bf16[64,3,3072]{2,1,0:T(4,128)(2,1)} %bitcast.7), calls=%async_computation | async-start | bytes 3145728 | tf_op jit(solution)/shard_map/all_to_all | solution.py:41
  28.5 38.4 %copy-start.24 = (f32[8,3072]{1,0:T(8,128)}, f32[8,3072]{1,0:T(8,128)S(1)}, u32[]{:S(2)}) copy-start(f32[8,3072]{1,0:T(8,128)S(1)} %bitcast_convert_fusion) | copy-start | bytes 294916
  57.0 41.0 %copy-start.1 = (f32[2,192,1024]{2,1,0:T(8,128)}, f32[2,192,1024]{2,1,0:T(8,128)S(1)}, u32[]{:S(2)}) copy-start(f32[2,192,1024]{2,1,0:T(8,128)S(1)} %get-tuple-element.57) | copy-start | bytes 4718596
  61.3 28.4 %all-to-all-start.1 = ((bf16[64,3,3072]{2,1,0:T(4,128)(2,1)}), bf16[64,3,3072]{2,1,0:T(4,128)(2,1)S(1)}, u32[]{:S(2)}, u32[]{:S(2)}) async-start(bf16[64,3,3072]{2,1,0:T(4,128)(2,1)} %reshape.574), calls=%async_computation.1 | async-start | bytes 3145728 | tf_op jit(solution)/shard_map/all_to_all | solution.py:48
  92.6 7.9 %collective-permute-start = (bf16[8,3072]{1,0:T(8,128)(2,1)S(1)}, bf16[8,3072]{1,0:T(8,128)(2,1)S(1)}, u32[]{:S(2)}, u32[]{:S(2)}) collective-permute-start(bf16[8,3072]{1,0:T(8,128)(2,1)S(1)} %fusion.158), channel_id=1, source_target_pairs={{0,64},{1,65},{2,66},{3,67},{4,68},{5,69},{6,70},{7,71},{8,72},{9,... | collective-permute-start | bytes 147464 | tf_op jit(solution)/shard_map/ppermute | solution.py:12
  104.1 29.1 %all-to-all-start.2 = ((bf16[64,3,3072]{2,1,0:T(4,128)(2,1)}), bf16[64,3,3072]{2,1,0:T(4,128)(2,1)}, u32[]{:S(2)}, u32[]{:S(2)}) async-start(bf16[64,3,3072]{2,1,0:T(4,128)(2,1)} %bitcast.17), calls=%async_computation.2 | async-start | bytes 3145728 | tf_op jit(solution)/shard_map/all_to_all | solution.py:41
  133.1 8.4 %slice-start.8 = ((s8[6291456]{0:T(1024)(128)(4,1)}), s8[2097152]{0:T(1024)(128)(4,1)S(1)}, s32[]{:S(2)}) async-start(s8[6291456]{0:T(1024)(128)(4,1)} %bitcast.557), calls=%async_computation.21 | async-start | bytes 4194304
  136.1 8.0 %slice-start.20 = ((s8[6291456]{0:T(1024)(128)(4,1)}), s8[4194304]{0:T(1024)(128)(4,1)S(1)}, s32[]{:S(2)}) async-start(s8[6291456]{0:T(1024)(128)(4,1)} %bitcast.597), calls=%async_computation.33 | async-start | bytes 8388608
  147.7 6.6 %copy-start.11 = (f32[2,192,1024]{2,1,0:T(8,128)S(1)}, f32[2,192,1024]{2,1,0:T(8,128)}, u32[]{:S(2)}) copy-start(f32[2,192,1024]{2,1,0:T(8,128)} %get-tuple-element.65) | copy-start | bytes 4718596
  147.7 28.5 %all-to-all-start.3 = ((bf16[64,3,3072]{2,1,0:T(4,128)(2,1)}), bf16[64,3,3072]{2,1,0:T(4,128)(2,1)S(1)}, u32[]{:S(2)}, u32[]{:S(2)}) async-start(bf16[64,3,3072]{2,1,0:T(4,128)(2,1)} %reshape.580), calls=%async_computation.3 | async-start | bytes 3145728 | tf_op jit(solution)/shard_map/all_to_all | solution.py:48
  155.3 23.5 %copy-start.53 = (s32[8,2]{0,1:T(2,128)S(1)}, s32[8,2]{0,1:T(2,128)}, u32[]{:S(2)}) copy-start(s32[8,2]{0,1:T(2,128)} %multiply_add_fusion.4) | copy-start | bytes 196
  155.3 29.8 %copy-start.4 = (f32[2,192,1024]{2,1,0:T(8,128)S(1)}, f32[2,192,1024]{2,1,0:T(8,128)}, u32[]{:S(2)}) copy-start(f32[2,192,1024]{2,1,0:T(8,128)} %copy-done.3) | copy-start | bytes 4718596
  177.6 9.2 %copy-start.41 = (bf16[1,8,3072]{2,1,0:T(8,128)(2,1)S(1)}, bf16[1,8,3072]{2,1,0:T(8,128)(2,1)}, u32[]{:S(2)}) copy-start(bf16[1,8,3072]{2,1,0:T(8,128)(2,1)} %constant_dynamic-slice_fusion.13) | copy-start | bytes 147460
  178.8 8.4 %copy-start.61 = (s32[16]{0:T(128)S(1)}, s32[16]{0:T(128)}, u32[]{:S(2)}) copy-start(s32[16]{0:T(128)} %multiply_add_fusion.9) | copy-start | bytes 196
  180.0 17.6 %copy-start.28 = (bf16[2,8,3072]{2,1,0:T(8,128)(2,1)}, bf16[2,8,3072]{2,1,0:T(8,128)(2,1)S(1)}, u32[]{:S(2)}) copy-start(bf16[2,8,3072]{2,1,0:T(8,128)(2,1)S(1)} %get-tuple-element.27) | copy-start | bytes 294916
  180.0 6.8 %collective-permute-start.1 = (bf16[8,3072]{1,0:T(8,128)(2,1)S(1)}, bf16[8,3072]{1,0:T(8,128)(2,1)S(1)}, u32[]{:S(2)}, u32[]{:S(2)}) collective-permute-start(bf16[8,3072]{1,0:T(8,128)(2,1)S(1)} %get-tuple-element.28), channel_id=1, source_target_pairs={{0,64},{1,65},{2,66},{3,67},{4,68},{5,69},{6,70},{7,71},{8,72},{9,... | collective-permute-start | bytes 147464 | tf_op jit(solution)/shard_map/ppermute | solution.py:12
  189.3 29.4 %all-to-all-start.4 = ((bf16[64,3,3072]{2,1,0:T(4,128)(2,1)}), bf16[64,3,3072]{2,1,0:T(4,128)(2,1)}, u32[]{:S(2)}, u32[]{:S(2)}) async-start(bf16[64,3,3072]{2,1,0:T(4,128)(2,1)} %bitcast.26), calls=%async_computation.4 | async-start | bytes 3145728 | tf_op jit(solution)/shard_map/all_to_all | solution.py:41
  218.6 8.4 %slice-start.10 = ((s8[6291456]{0:T(1024)(128)(4,1)}), s8[2097152]{0:T(1024)(128)(4,1)S(1)}, s32[]{:S(2)}) async-start(s8[6291456]{0:T(1024)(128)(4,1)} %bitcast.559), calls=%async_computation.23 | async-start | bytes 4194304
  221.6 8.1 %slice-start.22 = ((s8[6291456]{0:T(1024)(128)(4,1)}), s8[4194304]{0:T(1024)(128)(4,1)S(1)}, s32[]{:S(2)}) async-start(s8[6291456]{0:T(1024)(128)(4,1)} %bitcast.599), calls=%async_computation.35 | async-start | bytes 8388608
  233.2 28.4 %all-to-all-start.5 = ((bf16[64,3,3072]{2,1,0:T(4,128)(2,1)}), bf16[64,3,3072]{2,1,0:T(4,128)(2,1)S(1)}, u32[]{:S(2)}, u32[]{:S(2)}) async-start(bf16[64,3,3072]{2,1,0:T(4,128)(2,1)} %reshape.586), calls=%async_computation.5 | async-start | bytes 3145728 | tf_op jit(solution)/shard_map/all_to_all | solution.py:48
  240.3 22.2 %copy-start.52 = (s32[8,2]{0,1:T(2,128)S(1)}, s32[8,2]{0,1:T(2,128)}, u32[]{:S(2)}) copy-start(s32[8,2]{0,1:T(2,128)} %multiply_add_fusion.3) | copy-start | bytes 196
  240.4 22.4 %copy-start.18 = (f32[2,8,2,3072]{3,1,2,0:T(8,128)S(1)}, f32[2,8,2,3072]{3,1,2,0:T(8,128)}, u32[]{:S(2)}) copy-start(f32[2,8,2,3072]{3,1,2,0:T(8,128)} %copy-done.17) | copy-start | bytes 1179652
  240.4 22.4 %copy-start.35 = (f32[1,8,2,3072]{3,1,2,0:T(8,128)S(1)}, f32[1,8,2,3072]{3,1,2,0:T(8,128)}, u32[]{:S(2)}) copy-start(f32[1,8,2,3072]{3,1,2,0:T(8,128)} %constant_dynamic-slice_fusion.6) | copy-start | bytes 589828
  266.8 6.6 %copy-start.44 = (s32[1,1,8,2]{2,3,1,0:T(2,128)S(1)}, s32[1,1,8,2]{2,3,1,0:T(2,128)}, u32[]{:S(2)}) copy-start(s32[1,1,8,2]{2,3,1,0:T(2,128)} %get-tuple-element.39) | copy-start | bytes 196
  266.8 6.6 %copy-start.45 = (s32[1,1,8,2]{2,3,1,0:T(2,128)S(1)}, s32[1,1,8,2]{2,3,1,0:T(2,128)}, u32[]{:S(2)}) copy-start(s32[1,1,8,2]{2,3,1,0:T(2,128)} %get-tuple-element.44) | copy-start | bytes 196
  266.8 37.1 %slice-start = ((s8[6291456]{0:T(1024)(128)(4,1)}), s8[2097152]{0:T(1024)(128)(4,1)S(1)}, s32[]{:S(2)}) async-start(s8[6291456]{0:T(1024)(128)(4,1)} %bitcast.549), calls=%async_computation.13 | async-start | bytes 4194304
  266.8 29.2 %all-to-all-start.6 = ((bf16[64,3,3072]{2,1,0:T(4,128)(2,1)}), bf16[64,3,3072]{2,1,0:T(4,128)(2,1)}, u32[]{:S(2)}, u32[]{:S(2)}) async-start(bf16[64,3,3072]{2,1,0:T(4,128)(2,1)} %bitcast.568), calls=%async_computation.6 | async-start | bytes 3145728 | tf_op jit(solution)/shard_map/all_to_all | solution.py:41
  298.8 8.8 %slice-start.12 = ((s8[6291456]{0:T(1024)(128)(4,1)}), s8[4194304]{0:T(1024)(128)(4,1)S(1)}, s32[]{:S(2)}) async-start(s8[6291456]{0:T(1024)(128)(4,1)} %bitcast.561), calls=%async_computation.25 | async-start | bytes 8388608
  312.1 28.4 %all-to-all-start.7 = ((bf16[64,3,3072]{2,1,0:T(4,128)(2,1)}), bf16[64,3,3072]{2,1,0:T(4,128)(2,1)S(1)}, u32[]{:S(2)}, u32[]{:S(2)}) async-start(bf16[64,3,3072]{2,1,0:T(4,128)(2,1)} %reshape.592), calls=%async_computation.7 | async-start | bytes 3145728 | tf_op jit(solution)/shard_map/all_to_all | solution.py:48
  317.9 24.0 %copy-start.39 = (bf16[2,8,3072]{2,1,0:T(8,128)(2,1)S(1)}, bf16[2,8,3072]{2,1,0:T(8,128)(2,1)}, u32[]{:S(2)}) copy-start(bf16[2,8,3072]{2,1,0:T(8,128)(2,1)} %param.11) | copy-start | bytes 294916
  317.9 24.0 %copy-start.57 = (f32[8]{0:T(128)S(1)}, f32[8]{0:T(128)}, u32[]{:S(2)}) copy-start(f32[8]{0:T(128)} %copy-done.56) | copy-start | bytes 100
  317.9 24.0 %copy-start.63 = (f32[8]{0:T(128)S(1)}, f32[8]{0:T(128)}, u32[]{:S(2)}) copy-start(f32[8]{0:T(128)} %get-tuple-element.49) | copy-start | bytes 100
  342.1 7.5 %collective-permute-start.2 = (bf16[8,3072]{1,0:T(8,128)(2,1)S(1)}, bf16[8,3072]{1,0:T(8,128)(2,1)S(1)}, u32[]{:S(2)}, u32[]{:S(2)}) collective-permute-start(bf16[8,3072]{1,0:T(8,128)(2,1)S(1)} %get-tuple-element.18), channel_id=1, source_target_pairs={{64,0},{65,1},{66,2},{67,3},{68,4},{69,5},{70,6},{71,7},{72,8},{73... | collective-permute-start | bytes 147464 | tf_op jit(solution)/shard_map/ppermute | solution.py:12
  352.4 29.2 %all-to-all-start.8 = ((bf16[64,3,3072]{2,1,0:T(4,128)(2,1)}), bf16[64,3,3072]{2,1,0:T(4,128)(2,1)}, u32[]{:S(2)}, u32[]{:S(2)}) async-start(bf16[64,3,3072]{2,1,0:T(4,128)(2,1)} %bitcast.68), calls=%async_computation.8 | async-start | bytes 3145728 | tf_op jit(solution)/shard_map/all_to_all | solution.py:41
  358.6 32.3 %slice-start.2 = ((s8[6291456]{0:T(1024)(128)(4,1)}), s8[2097152]{0:T(1024)(128)(4,1)S(1)}, s32[]{:S(2)}) async-start(s8[6291456]{0:T(1024)(128)(4,1)} %bitcast.551), calls=%async_computation.15 | async-start | bytes 4194304
  385.5 9.1 %slice-start.14 = ((s8[6291456]{0:T(1024)(128)(4,1)}), s8[4194304]{0:T(1024)(128)(4,1)S(1)}, s32[]{:S(2)}) async-start(s8[6291456]{0:T(1024)(128)(4,1)} %bitcast.563), calls=%async_computation.27 | async-start | bytes 8388608
  399.1 28.4 %all-to-all-start.9 = ((bf16[64,3,3072]{2,1,0:T(4,128)(2,1)}), bf16[64,3,3072]{2,1,0:T(4,128)(2,1)S(1)}, u32[]{:S(2)}, u32[]{:S(2)}) async-start(bf16[64,3,3072]{2,1,0:T(4,128)(2,1)} %reshape.598), calls=%async_computation.9 | async-start | bytes 3145728 | tf_op jit(solution)/shard_map/all_to_all | solution.py:48
  404.0 162.1 %all-gather.3.cloned.1.call-start = ((), (), s32[]{:S(2)}) async-start(), calls=%async_computation.12 | async-start | bytes 6389760 | tf_op jit(solution)/shard_map/all_gather | solution.py:222
  428.1 8.4 %copy-start.31 = (f32[1,8,2,3072]{3,1,2,0:T(8,128)S(1)}, f32[1,8,2,3072]{3,1,2,0:T(8,128)}, u32[]{:S(2)}) copy-start(f32[1,8,2,3072]{3,1,2,0:T(8,128)} %get-tuple-element.29) | copy-start | bytes 589828
  429.0 7.5 %collective-permute-start.3 = (bf16[8,3072]{1,0:T(8,128)(2,1)S(1)}, bf16[8,3072]{1,0:T(8,128)(2,1)S(1)}, u32[]{:S(2)}, u32[]{:S(2)}) collective-permute-start(bf16[8,3072]{1,0:T(8,128)(2,1)S(1)} %get-tuple-element.12), channel_id=1, source_target_pairs={{64,0},{65,1},{66,2},{67,3},{68,4},{69,5},{70,6},{71,7},{72,8},{73... | collective-permute-start | bytes 147464 | tf_op jit(solution)/shard_map/ppermute | solution.py:12
  439.8 41.8 %slice-start.4 = ((s8[6291456]{0:T(1024)(128)(4,1)}), s8[2097152]{0:T(1024)(128)(4,1)S(1)}, s32[]{:S(2)}) async-start(s8[6291456]{0:T(1024)(128)(4,1)} %bitcast.553), calls=%async_computation.17 | async-start | bytes 4194304
  476.1 9.2 %slice-start.16 = ((s8[6291456]{0:T(1024)(128)(4,1)}), s8[4194304]{0:T(1024)(128)(4,1)S(1)}, s32[]{:S(2)}) async-start(s8[6291456]{0:T(1024)(128)(4,1)} %bitcast.565), calls=%async_computation.29 | async-start | bytes 8388608
  489.8 32.2 %all-to-all-start.11 = ((bf16[64,3,3072]{2,1,0:T(4,128)(2,1)}), bf16[64,3,3072]{2,1,0:T(4,128)(2,1)S(1)}, u32[]{:S(2)}, u32[]{:S(2)}) async-start(bf16[64,3,3072]{2,1,0:T(4,128)(2,1)} %reshape.604), calls=%async_computation.11 | async-start | bytes 3145728 | tf_op jit(solution)/shard_map/all_to_all | solution.py:48
  495.4 27.6 %copy-start.43 = (bf16[1,2,8,3072]{3,2,1,0:T(8,128)(2,1)}, bf16[1,2,8,3072]{3,2,1,0:T(8,128)(2,1)S(1)}, u32[]{:S(2)}) copy-start(bf16[1,2,8,3072]{3,2,1,0:T(8,128)(2,1)S(1)} %fusion.175) | copy-start | bytes 294916
  523.5 46.4 %copy-start.42 = (bf16[1,2,8,3072]{3,2,1,0:T(8,128)(2,1)}, bf16[1,2,8,3072]{3,2,1,0:T(8,128)(2,1)S(1)}, u32[]{:S(2)}) copy-start(bf16[1,2,8,3072]{3,2,1,0:T(8,128)(2,1)S(1)} %fusion.187) | copy-start | bytes 294916
  (56 other events, 214.5 us)
Sparse Core Ops, SparseCore 0:
  438.2 127.9 all-gather.2
